TPU v7x, 32 devices: a whole 2x2x4 slice. The times are simulated.
32 devices in a mesh: inp: 8 (over z, core), tm: 4 (over y, x).
Axes of the slice: x: 2, y: 2, z: 4, core: 2. Of those that a mesh axis runs over, the one named last changes fastest.
Arguments:
- samples: bfloat16 [256, 786432], P('inp', 'tm'), may hold values from -6 to 6
- tap_weights: float32 [4, 512], replicated, may hold values from -3 to 3
Outputs:
- visibilities: float32 [256, 2, 256, 256], P('tm', None, 'inp')
All inputs are finite; a program needn't handle non-finite values.
Results may differ from a plain program's by a relative error of at most 0.00081.
Values may be sent and summed in bfloat16 or wider, within the bound.
A program may use at most 128 MiB of HBM per device.

v0:
```python
import functools
import math

import jax
import jax.numpy as jnp
import numpy as np
from jax import lax
from jax.experimental import pallas as pl
from jax.experimental.pallas import tpu as pltpu
from jax.sharding import PartitionSpec as P

MESH = pl.DeviceIdType.MESH
STEPS = 16
AHEAD = 4


def passed_along(block, axis, distance):
    devices = range(lax.axis_size(axis))
    route = [(i - distance, i) for i in devices if i - distance in devices]
    return lax.ppermute(block, axis, route)


def filter_taps(extended, weights, count):
    total = weights[0][None, None, :] * extended[:, 0:count, :].astype(jnp.float32)
    for tap in range(1, weights.shape[0]):
        total = total + weights[tap][None, None, :] * extended[:, tap : tap + count, :].astype(
            jnp.float32
        )
    return total


def exchange_and_correlate(
    n_inp, n_tm, steps, scale, even, odd, out, recv, part, got, send_sem, recv_sem, own_sem, put_sem, got_sem
):
    me = lax.axis_index("inp")
    seg = lax.axis_index("tm")
    ch_dev, _, _, in_dev, count = recv.shape
    per = ch_dev // steps
    inputs = n_inp * in_dev
    rows = inputs // n_tm
    fold = ch_dev // 2
    turn = steps // 2

    barrier = pltpu.get_barrier_semaphore()
    for d in range(1, n_inp):
        pl.semaphore_signal(
            barrier, inc=1, device_id={"inp": lax.rem(me + d, n_inp)}, device_id_type=MESH
        )
    for d in range(1, n_tm):
        pl.semaphore_signal(
            barrier, inc=1, device_id={"tm": lax.rem(seg + d, n_tm)}, device_id_type=MESH
        )
    pl.semaphore_wait(barrier, n_inp - 1 + n_tm - 1)

    def own_copy(g, spec=even, at=0):
        return pltpu.make_async_copy(
            spec.at[me, pl.ds(at * per, per)], recv.at[pl.ds(g * per, per), :, me], own_sem.at[g]
        )

    def turn_copy(g, d, spec=even, at=0):
        peer = lax.rem(me + d, n_inp)
        return pltpu.make_async_remote_copy(
            src_ref=spec.at[peer, pl.ds(at * per, per)],
            dst_ref=recv.at[pl.ds(g * per, per), :, me],
            send_sem=send_sem.at[g, d - 1],
            recv_sem=recv_sem.at[g, d - 1],
            device_id={"inp": peer},
            device_id_type=MESH,
        )

    def sum_copy(g, d):
        chunk = pl.ds(g * per, per)
        peer = lax.rem(seg + d, n_tm)
        return pltpu.make_async_remote_copy(
            src_ref=part.at[peer, chunk],
            dst_ref=got.at[d - 1, chunk],
            send_sem=put_sem.at[g, d - 1],
            recv_sem=got_sem.at[g, d - 1],
            device_id={"tm": peer},
            device_id_type=MESH,
        )

    def each(first, end, body):
        def step(d, carry):
            body(d)
            return carry

        lax.fori_loop(first, end, step, 0)

    def send_from(g, spec, at):
        own_copy(g, spec, at).start()
        first = n_inp // 2 - 1
        each(
            0,
            n_inp - 1,
            lambda k: turn_copy(g, 1 + lax.rem(k + first, n_inp - 1), spec, at).start(),
        )

    def send(g):
        @pl.when(g < turn)
        def _():
            send_from(g, even, g)

        @pl.when(g >= turn)
        def _():
            send_from(g, odd, g - turn)

    def side(ch, p):
        block = recv[ch, p]
        if in_dev % 16 == 0:
            return block.reshape(inputs, count)
        return block.astype(jnp.float32).reshape(inputs, count).astype(jnp.bfloat16)

    def correlate(ch):
        real = side(ch, 0)
        imag = side(ch, 1)
        x = jnp.concatenate([real, imag], axis=1)
        y = jnp.concatenate([imag, -real], axis=1)
        for p, left in ((0, x), (1, y)):
            product = lax.dot_general(
                left, x, (((1,), (1,)), ((), ())), preferred_element_type=jnp.float32
            )
            for q in range(n_tm):
                part[q, ch, p] = product[q * rows : (q + 1) * rows]

    def finish(g):
        each(1, n_tm, lambda d: sum_copy(g, d).wait_recv())

        def add(k):
            ch = g * per + k
            total = part[seg, ch]
            for d in range(1, n_tm):
                total = total + got[d - 1, ch]
            out[lax.rem(ch, fold) * 2 + ch // fold] = total * scale

        each(0, per, add)

    for g in range(min(AHEAD, steps)):
        send(g)

    def step(g):
        @pl.when(g + AHEAD < steps)
        def _():
            send(g + AHEAD)

        own_copy(g).wait()
        each(1, n_inp, lambda d: turn_copy(g, d).wait_recv())
        each(0, per, lambda k: correlate(g * per + k))
        each(1, n_tm, lambda d: sum_copy(g, d).start())

        @pl.when(g >= 1)
        def _():
            finish(g - 1)

    each(0, steps, step)
    finish(steps - 1)

    def drain(g):
        each(1, n_inp, lambda d: turn_copy(g, d).wait_send())
        each(1, n_tm, lambda d: sum_copy(g, d).wait_send())

    each(0, steps, drain)


def per_device(samples, tap_weights):
    in_dev = samples.shape[0]
    frame = tap_weights.shape[1]
    taps = tap_weights.shape[0]
    rim = taps - 1
    spectra_dev = samples.shape[1] // frame
    frames = samples.reshape(in_dev, spectra_dev, frame)
    before = passed_along(frames[:, spectra_dev - rim :, :], "tm", 1)
    filtered = filter_taps(jnp.concatenate([before, frames], axis=1), tap_weights, spectra_dev)
    n_inp = lax.axis_size("inp")
    n_tm = lax.axis_size("tm")
    ch_dev = frame // 2 // n_inp
    fold = frame // 2
    low, high = filtered[:, :, :fold], filtered[:, :, fold:]
    sides = []
    for odd, folded in ((0, low + high), (1, low - high)):
        column = np.arange(fold)
        channel = column // 2 * 2 + odd
        phase = np.arange(fold)[:, None] * channel[None, :] % frame
        angle = phase * (2.0 * math.pi / frame)
        table = np.where(column % 2 == 0, np.cos(angle), -np.sin(angle)) * frame ** (-0.5)
        side = jnp.einsum(
            "isn,nj->ijs",
            folded,
            jnp.asarray(table, jnp.float32),
            precision=lax.Precision.HIGH,
            preferred_element_type=jnp.float32,
        ).astype(jnp.bfloat16)
        side = side.reshape(in_dev, n_inp, ch_dev // 2, 2, spectra_dev)
        sides.append(side.transpose(1, 2, 3, 0, 4))
    steps = math.gcd(STEPS, ch_dev)
    inputs = n_inp * in_dev
    rows = inputs // n_tm
    scale = 1.0 / math.sqrt(spectra_dev * n_tm)
    mine = pl.pallas_call(
        functools.partial(exchange_and_correlate, n_inp, n_tm, steps, scale),
        out_shape=jax.ShapeDtypeStruct((ch_dev, 2, rows, inputs), jnp.float32),
        in_specs=[pl.BlockSpec(memory_space=pltpu.HBM)] * 2,
        out_specs=pl.BlockSpec(memory_space=pltpu.VMEM),
        scratch_shapes=[
            pltpu.VMEM((ch_dev, 2, n_inp, in_dev, spectra_dev), jnp.bfloat16),
            pltpu.VMEM((n_tm, ch_dev, 2, rows, inputs), jnp.float32),
            pltpu.VMEM((n_tm - 1, ch_dev, 2, rows, inputs), jnp.float32),
            pltpu.SemaphoreType.DMA((steps, n_inp - 1)),
            pltpu.SemaphoreType.DMA((steps, n_inp - 1)),
            pltpu.SemaphoreType.DMA((steps,)),
            pltpu.SemaphoreType.DMA((steps, n_tm - 1)),
            pltpu.SemaphoreType.DMA((steps, n_tm - 1)),
        ],
        compiler_params=pltpu.CompilerParams(
            collective_id=0, has_side_effects=True, vmem_limit_bytes=60 << 20
        ),
    )(*sides)
    return mine.transpose(2, 1, 0, 3)


def solution(mesh):
    return jax.shard_map(
        per_device,
        mesh=mesh,
        in_specs=(P("inp", "tm"), P()),
        out_specs=P("tm", None, "inp", None),
        check_vma=False,
    )
```

profile of v0, /device:TPU:28, one launch (start us, length us, event | category | flops | bytes accessed | tf_op | source)
XLA Modules:
  0.0 382.7 jit_solution(3143837995247611782)
XLA Ops:
  0.0 0.0 copy-start.2
  0.0 9.3 %copy.8 = bf16[4,8,384,512]{3,2,1,0:T(8,128)(2,1)S(1)} copy(bf16[4,8,384,512]{3,1,2,0:T(8,128)(2,1)} %bitcast.26) | data formatting | bytes 25165824
  9.3 0.0 copy-start
  9.4 0.1 slice.40
  9.4 3.4 collective-permute-start
  12.8 0.0 copy-done.2
  12.9 4.6 %collective-permute-done = bf16[32,3,512]{2,1,0:T(4,128)(2,1)S(1)} collective-permute-done((bf16[32,3,512]{2,1,0:T(4,128)(2,1)S(1)}, bf16[32,3,512]{2,1,0:T(4,128)(2,1)S(1)}, u32[]{:S(2)}, u32[]{:S(2)}) %collective-permute-start) | collective-permute-done | bytes 98336 | tf_op jit(solution)/shard_map/ppermute | solution.py:20
  17.5 0.0 copy-start.1
  17.5 15.0 %multiply_add_fusion = f32[32,384,512]{2,1,0:T(8,128)} fusion(bf16[32,384,512]{2,1,0:T(8,128)(2,1)S(1)} %bitcast.22, bf16[32,3,512]{2,1,0:T(4,128)(2,1)S(1)} %collective-permute-done, f32[512]{0:T(512)S(1)} %bitcast.29, f32[512]{0:T(512)S(1)} %bitcast.30, f32[512]{0:T(512)S(1)} %bitcast.28, f32[512]{0:T(512)S(1)} %bitcast.27), kind=kLoop, calls=%fused_computation | loop fusion | flops 125829120 | bytes 37855232 | tf_op jit(solution)/shard_map/add | solution.py:26
  32.4 0.0 copy-done
  32.4 10.9 %convert_bitcast_fusion.1 = bf16[32,256,384]{2,1,0:T(8,128)(2,1)S(1)} fusion(f32[256,256,1]{0,1,2:T(8,128)S(1)} %copy-done, f32[32,384,512]{2,1,0:T(8,128)} %multiply_add_fusion), kind=kOutput, calls=%fused_computation.15 | convolution fusion | flops 4838129664 | bytes 31719424 | tf_op jit(solution)/shard_map/isn,nj->ijs/dot_general | solution.py:186
  43.4 0.0 copy-done.1
  43.4 12.7 %convert_bitcast_fusion = bf16[32,256,384]{2,1,0:T(8,128)(2,1)} fusion(f32[256,256,1]{0,1,2:T(8,128)S(1)} %copy-done.1, f32[32,384,512]{2,1,0:T(8,128)} %multiply_add_fusion), kind=kOutput, calls=%fused_computation.14 | convolution fusion | flops 4838129664 | bytes 31719424 | tf_op jit(solution)/shard_map/isn,nj->ijs/dot_general | solution.py:186
  56.1 9.1 %copy.6 = bf16[32,256,384]{2,0,1:T(8,128)(2,1)} copy(bf16[32,256,384]{2,1,0:T(8,128)(2,1)} %convert_bitcast_fusion) | data formatting | bytes 12582912 | tf_op jit(solution)/shard_map/convert_element_type | solution.py:192
  65.2 6.4 %copy.5 = bf16[32,256,384]{2,0,1:T(8,128)(2,1)} copy(bf16[32,256,384]{2,1,0:T(8,128)(2,1)S(1)} %convert_bitcast_fusion.1) | data formatting | bytes 12582912 | tf_op jit(solution)/shard_map/convert_element_type | solution.py:192
  71.6 304.4 %shard_map.46 = f32[32,2,64,256]{3,2,1,0:T(8,128)} custom-call(bf16[8,16,2,32,384]{4,3,2,1,0:T(8,128)(2,1)} %bitcast.24, bf16[8,16,2,32,384]{4,3,2,1,0:T(8,128)(2,1)} %bitcast.23), custom_call_target="tpu_custom_call" | custom-call | tf_op jit(solution)/shard_map/pallas_call | solution.py:199
  376.1 6.6 %copy.7 = f32[64,2,32,256]{3,2,1,0:T(8,128)} copy(f32[64,2,32,256]{3,0,1,2:T(8,128)} %bitcast.25) | data formatting | bytes 8388608 | tf_op jit(solution)/shard_map/transpose | solution.py:218
  (1 shorter events, 0.0 us)
Async XLA Ops:
  0.0 12.8 %copy-start.2 = (f32[4,512]{1,0:T(4,128)S(1)}, f32[4,512]{1,0:T(4,128)}, u32[]{:S(2)}) copy-start(f32[4,512]{1,0:T(4,128)} %param.5) | copy-start | bytes 24580
  9.3 23.1 %copy-start = (f32[256,256,1]{0,1,2:T(8,128)S(1)}, f32[256,256,1]{0,1,2:T(8,128)}, u32[]{:S(2)}) copy-start(f32[256,256,1]{0,1,2:T(8,128)} %constant.6) | copy-start | bytes 786436
  9.4 8.0 %collective-permute-start = (bf16[32,3,512]{2,1,0:T(4,128)(2,1)S(1)}, bf16[32,3,512]{2,1,0:T(4,128)(2,1)S(1)}, u32[]{:S(2)}, u32[]{:S(2)}) collective-permute-start(bf16[32,3,512]{2,1,0:T(4,128)(2,1)S(1)} %slice.40), channel_id=1, source_target_pairs={{0,1},{1,2},{2,3},{4,5},{5,6},{6,7},{8,9},{9,10},{10,11},{12,13},{... | collective-permute-start | bytes 294920 | tf_op jit(solution)/shard_map/ppermute | solution.py:20
  17.5 25.9 %copy-start.1 = (f32[256,256,1]{0,1,2:T(8,128)S(1)}, f32[256,256,1]{0,1,2:T(8,128)}, u32[]{:S(2)}) copy-start(f32[256,256,1]{0,1,2:T(8,128)} %constant.7) | copy-start | bytes 786436
where the time goes:
time: 387 us; the launch traced here: 383 us
  Pallas kernels  304 us (79%)
  local copies, waits for them, and re-layouts  31.6 us (8%)
  matrix products  23.6 us (6%)
  other arithmetic  15 us (4%)
  waiting for transfers between devices  4.6 us (1%)
    pallas_call x1, Pallas kernels, per_device(): pl.pallas_call(functools.partial(exchange_and_correlate, n_inp, n_tm, ste...  304 us
    dot_general x2, matrix products, per_device(): jnp.einsum('isn,nj->ijs', folded, jnp.asarray(table, jnp.float32), precis...  23.6 us
    convert_element_type x2, local copies, waits for them, and re-layouts, per_device(): side = jnp.einsum('isn,nj->ijs', folded, jnp.asarray(table, jnp.float32),...  15.6 us
    add x1, other arithmetic, filter_taps(): total + weights[tap][None, None, :] * extended[:, tap:tap + count, :].ast...  15 us
    unnamed x7, local copies, waits for them, and re-layouts  9.35 us
  transfers between devices with their start and end apart: 1, of which 1 were waited for; matrix products, arithmetic and copies ran while one was open for 0% of the time, Pallas kernels for 0%

commit v1 on v0

v1 whole, which is shorter than its diff:
```python
import functools
import math

import jax
import jax.numpy as jnp
import numpy as np
from jax import lax
from jax.experimental import pallas as pl
from jax.experimental.pallas import tpu as pltpu
from jax.sharding import PartitionSpec as P

MESH = pl.DeviceIdType.MESH
HEAD = 4
STEPS = 32
AHEAD = 10
LAG = 3
RING = 8
LANES = 128


def each(first, end, body):
    def step(d, carry):
        body(d)
        return carry

    lax.fori_loop(first, end, step, 0)


def across(me, mask, n):
    if n & (n - 1):
        return lax.rem(me + mask, n), lax.rem(me + n - mask, n)
    peer, bit = me, 1
    while bit < n:
        flip = lax.rem(mask // bit, 2)
        peer = peer + flip * bit * (1 - 2 * lax.rem(me // bit, 2))
        bit *= 2
    return peer, peer


def correlator(
    n_inp, n_tm, scale, x, weights, table_hbm, out,
    xb, halo, table, low, high, turn, spec, recv, part, got, held,
    x_sem, table_sem, halo_sem, send_sem, recv_sem, own_sem, put_sem, got_sem, out_sem,
):
    me = lax.axis_index("inp")
    seg = lax.axis_index("tm")
    ch_dev, _, _, in_dev, count = recv.shape
    groups, _, _, frame = halo.shape
    rim = halo.shape[1]
    pack = xb.shape[1]
    block = xb.shape[2] - rim
    width = pack * 8
    half = frame // 2
    fold = ch_dev // 2
    inputs = n_inp * in_dev
    rows = inputs // n_tm
    head = max(ch_dev // HEAD, 1)
    per = max(ch_dev // STEPS, 1)
    chunks = 1 + (ch_dev - head) // per
    in_units = in_dev // width
    s_units = count // block
    units = in_units * s_units

    barrier = pltpu.get_barrier_semaphore()
    for d in range(1, n_inp):
        pl.semaphore_signal(
            barrier, inc=1, device_id={"inp": lax.rem(me + d, n_inp)}, device_id_type=MESH
        )
    for d in range(1, n_tm):
        pl.semaphore_signal(
            barrier, inc=1, device_id={"tm": lax.rem(seg + d, n_tm)}, device_id_type=MESH
        )

    def place(u):
        return lax.rem(u, in_units), lax.rem(u // in_units + 1, s_units)

    def inner_load(u):
        g, s = place(u)
        slot = lax.rem(u, 2)
        return pltpu.make_async_copy(
            x.at[pl.ds(g * pack, pack), pl.ds(s * block - rim, block + rim)],
            xb.at[slot], x_sem.at[slot],
        )

    def first_load(u):
        g, _ = place(u)
        slot = lax.rem(u, 2)
        return pltpu.make_async_copy(
            x.at[pl.ds(g * pack, pack), pl.ds(0, block)],
            xb.at[slot, :, pl.ds(rim, block)], x_sem.at[slot],
        )

    def load(u, act):
        _, s = place(u)

        @pl.when(s > 0)
        def _():
            act(inner_load(u))

        @pl.when(s == 0)
        def _():
            act(first_load(u))

    def rim_copy():
        return pltpu.make_async_remote_copy(
            src_ref=x.at[:, pl.ds(count - rim, rim)],
            dst_ref=halo,
            send_sem=halo_sem.at[0],
            recv_sem=halo_sem.at[1],
            device_id={"tm": lax.rem(seg + 1, n_tm)},
            device_id_type=MESH,
        )

    table_copy = pltpu.make_async_copy(table_hbm, table, table_sem.at[0])
    load(0, lambda copy: copy.start())
    table_copy.start()

    def own_head():
        return pltpu.make_async_copy(
            spec.at[me, pl.ds(0, head)], recv.at[pl.ds(0, head), :, me], own_sem.at[0]
        )

    def own_copy(c):
        chunk = pl.ds(head + (c - 1) * per, per)
        return pltpu.make_async_copy(
            spec.at[me, chunk], recv.at[chunk, :, me], own_sem.at[c]
        )

    def remote(mask, c, src, dst):
        return pltpu.make_async_remote_copy(
            src_ref=src,
            dst_ref=dst,
            send_sem=send_sem.at[c, mask - 1],
            recv_sem=recv_sem.at[c, mask - 1],
            device_id={"inp": across(me, mask, n_inp)[0]},
            device_id_type=MESH,
        )

    def unit_copy(u, mask):
        g, s = place(u)
        peer = across(me, mask, n_inp)[0]
        at = pl.ds(pl.multiple_of(g * width, width), width)
        span = pl.ds(pl.multiple_of(s * block, block), block)
        first = pl.ds(0, head)
        return remote(
            mask, 0, spec.at[peer, first, :, at, span], recv.at[first, :, me, at, span]
        )

    def head_copy(mask):
        peer = across(me, mask, n_inp)[0]
        first = pl.ds(0, head)
        return remote(mask, 0, spec.at[peer, first], recv.at[first, :, me])

    def chunk_copy(c, mask):
        peer = across(me, mask, n_inp)[0]
        chunk = pl.ds(head + (c - 1) * per, per)
        return remote(mask, c, spec.at[peer, chunk], recv.at[chunk, :, me])

    def send(c):
        own_copy(c).start()
        each(0, n_inp - 1, lambda k: chunk_copy(c, n_inp - 1 - k).start())

    def filter_unit(u):
        slot = lax.rem(u, 2)
        step = 8

        def some(k):
            g = k // (block // step)
            s = lax.rem(k, block // step) * step
            to = pl.ds(pl.multiple_of((g * block + s) * 8, step * 8), step * 8)
            for t in range(half // LANES):
                sides = []
                for first in (t * LANES, half + t * LANES):
                    lane = slice(first, first + LANES)
                    frames = xb[slot, g, pl.ds(s, step + rim), :, lane].astype(jnp.float32)
                    total = weights[0:1, lane][None] * frames[0:step]
                    for tap in range(1, rim + 1):
                        total = total + weights[tap : tap + 1, lane][None] * frames[tap : tap + step]
                    sides.append(total.reshape(step * 8, LANES))
                low[t, to] = sides[0] + sides[1]
                high[t, to] = sides[0] - sides[1]

        each(0, pack * (block // step), some)

    def transform(folded, odd):
        def pair(k):
            two = []
            for i in (2 * k, 2 * k + 1):
                at = (i // 8) * (block * 8) + lax.rem(i, 8)
                two.append(
                    jnp.concatenate(
                        [folded[t, pl.ds(at, block, stride=8), :] for t in range(half // LANES)],
                        axis=1,
                    )
                )
            value = jnp.concatenate(two, axis=0)
            top = value.astype(jnp.bfloat16)
            rest = (value - top.astype(jnp.float32)).astype(jnp.bfloat16)
            side = lax.dot_general(
                table[odd],
                jnp.concatenate([top, top, rest], axis=1),
                (((1,), (1,)), ((), ())),
                preferred_element_type=jnp.float32,
            )
            for n in range(2):
                turn[pl.ds(2 * k + n, half, stride=width), :] = side[:, n * block : (n + 1) * block]

        each(0, width // 2, pair)

    def spread(u, odd):
        g, s = place(u)
        at = pl.ds(pl.multiple_of(g * width, width), width)
        span = pl.ds(pl.multiple_of(s * block, block), block)
        size = 2 * width

        def some(k):
            rows_in = turn[pl.ds(pl.multiple_of(k * size, size), size), :]
            spec[k // fold, odd * fold + lax.rem(k, fold), :, at, span] = rows_in.astype(
                jnp.bfloat16
            ).reshape(2, width, block)

        each(0, n_inp * fold, some)

    def unit(u):
        @pl.when(u + 1 < units)
        def _():
            load(u + 1, lambda copy: copy.start())

        load(u, lambda copy: copy.wait())
        g, s = place(u)

        @pl.when(s == 0)
        def _():
            @pl.when(jnp.logical_and(seg > 0, u == units - in_units))
            def _():
                rim_copy().wait_recv()

            @pl.when(jnp.logical_and(seg == 0, u == units - in_units))
            def _():
                halo[...] = jnp.zeros_like(halo)

            xb[lax.rem(u, 2), :, 0:rim] = halo[pl.ds(g * pack, pack)]

        filter_unit(u)

        @pl.when(u == 0)
        def _():
            table_copy.wait()

        transform(low, 0)
        spread(u, 0)

        @pl.when(u == 0)
        def _():
            pl.semaphore_wait(barrier, n_inp - 1 + n_tm - 1)

            @pl.when(seg + 1 < n_tm)
            def _():
                rim_copy().start()

        each(0, n_inp - 1, lambda k: unit_copy(u, n_inp - 1 - k).start())
        transform(high, 1)
        spread(u, 1)

    each(0, units, unit)
    own_head().start()

    @pl.when(seg + 1 < n_tm)
    def _():
        rim_copy().wait_send()

    def sum_copy(g, d):
        peer = lax.rem(seg + d, n_tm)
        return pltpu.make_async_remote_copy(
            src_ref=part.at[lax.rem(g, RING), peer],
            dst_ref=got.at[d - 1, g],
            send_sem=put_sem.at[g, d - 1],
            recv_sem=got_sem.at[g, d - 1],
            device_id={"tm": peer},
            device_id_type=MESH,
        )

    def side(ch, p):
        value = recv[ch, p]
        if in_dev % 16 == 0:
            return value.reshape(inputs, count)
        return value.astype(jnp.float32).reshape(inputs, count).astype(jnp.bfloat16)

    def correlate(ch):
        real = side(ch, 0)
        imag = side(ch, 1)
        a = jnp.concatenate([real, imag], axis=1)
        b = jnp.concatenate([imag, -real], axis=1)
        for p, left in ((0, a), (1, b)):
            product = lax.dot_general(
                left, a, (((1,), (1,)), ((), ())), preferred_element_type=jnp.float32
            )
            for q in range(n_tm):
                part[lax.rem(ch, RING), q, p] = product[q * rows : (q + 1) * rows]

    def finish(g):
        each(1, n_tm, lambda d: sum_copy(g, d).wait_recv())
        ch = lax.rem(g, fold) * 2 + g // fold
        for p in range(2):
            total = part[lax.rem(g, RING), seg, p]
            for d in range(1, n_tm):
                total = total + got[d - 1, g, p]
            total = total * scale
            for t in range(inputs // LANES):
                at = pl.ds(p * ch_dev + ch, rows, stride=2 * ch_dev)
                held[t, at, :] = total[:, t * LANES : (t + 1) * LANES]

    def channel(g):
        @pl.when(g >= RING)
        def _():
            each(1, n_tm, lambda d: sum_copy(g - RING, d).wait_send())

        correlate(g)
        each(1, n_tm, lambda d: sum_copy(g, d).start())

        @pl.when(g >= LAG)
        def _():
            finish(g - LAG)

    for c in range(1, min(AHEAD, chunks)):
        send(c)
    own_head().wait()
    each(1, n_inp, lambda mask: head_copy(mask).wait_recv())
    each(0, head, channel)

    def step(c):
        @pl.when(c + AHEAD - 1 < chunks)
        def _():
            send(c + AHEAD - 1)

        own_copy(c).wait()
        each(1, n_inp, lambda mask: chunk_copy(c, mask).wait_recv())
        each(0, per, lambda k: channel(head + (c - 1) * per + k))

    each(1, chunks, step)
    each(max(ch_dev - LAG, 0), ch_dev, finish)
    out_copies = [
        pltpu.make_async_copy(held.at[t], out.at[:, pl.ds(t * LANES, LANES)], out_sem.at[t])
        for t in range(inputs // LANES)
    ]
    for copy in out_copies:
        copy.start()
    each(1, n_inp, lambda mask: head_copy(mask).wait_send())
    each(1, chunks, lambda c: each(1, n_inp, lambda mask: chunk_copy(c, mask).wait_send()))
    each(
        max(ch_dev - RING, 0),
        ch_dev,
        lambda g: each(1, n_tm, lambda d: sum_copy(g, d).wait_send()),
    )
    for copy in out_copies:
        copy.wait()


def tables(frame):
    fold = frame // 2
    sides = []
    for odd in (0, 1):
        column = np.arange(fold)
        channel = column // 2 * 2 + odd
        phase = np.arange(fold)[:, None] * channel[None, :] % frame
        angle = phase * (2.0 * math.pi / frame)
        whole = np.where(column % 2 == 0, np.cos(angle), -np.sin(angle)) * frame ** (-0.5)
        whole = whole.T.astype(np.float32)
        top = whole.astype(jnp.bfloat16)
        rest = (whole - top.astype(np.float32)).astype(jnp.bfloat16)
        sides.append(np.concatenate([top, rest, top], axis=1))
    return np.stack(sides)


def per_device(samples, tap_weights):
    in_dev = samples.shape[0]
    taps, frame = tap_weights.shape
    rim = taps - 1
    count = samples.shape[1] // frame
    n_inp = lax.axis_size("inp")
    n_tm = lax.axis_size("tm")
    ch_dev = frame // 2 // n_inp
    inputs = n_inp * in_dev
    rows = inputs // n_tm
    groups = in_dev // 8
    pack = math.gcd(groups, 2)
    block = LANES
    head = max(ch_dev // HEAD, 1)
    per = max(ch_dev // STEPS, 1)
    chunks = 1 + (ch_dev - head) // per
    scale = 1.0 / math.sqrt(count * n_tm)
    frames = samples.reshape(groups, 8, count, frame).transpose(0, 2, 1, 3)
    mine = pl.pallas_call(
        functools.partial(correlator, n_inp, n_tm, scale),
        out_shape=jax.ShapeDtypeStruct((rows * 2 * ch_dev, inputs), jnp.float32),
        in_specs=[
            pl.BlockSpec(memory_space=pltpu.HBM),
            pl.BlockSpec(memory_space=pltpu.VMEM),
            pl.BlockSpec(memory_space=pltpu.HBM),
        ],
        out_specs=pl.BlockSpec(memory_space=pltpu.HBM),
        scratch_shapes=[
            pltpu.VMEM((2, pack, block + rim, 8, frame), jnp.bfloat16),
            pltpu.VMEM((groups, rim, 8, frame), jnp.bfloat16),
            pltpu.VMEM((2, frame // 2, 3 * (frame // 2)), jnp.bfloat16),
            pltpu.VMEM((frame // 2 // LANES, pack * block * 8, LANES), jnp.float32),
            pltpu.VMEM((frame // 2 // LANES, pack * block * 8, LANES), jnp.float32),
            pltpu.VMEM((frame // 2 * pack * 8, block), jnp.float32),
            pltpu.VMEM((n_inp, ch_dev, 2, in_dev, count), jnp.bfloat16),
            pltpu.VMEM((ch_dev, 2, n_inp, in_dev, count), jnp.bfloat16),
            pltpu.VMEM((RING, n_tm, 2, rows, inputs), jnp.float32),
            pltpu.VMEM((n_tm - 1, ch_dev, 2, rows, inputs), jnp.float32),
            pltpu.VMEM((inputs // LANES, rows * 2 * ch_dev, LANES), jnp.float32),
            pltpu.SemaphoreType.DMA((2,)),
            pltpu.SemaphoreType.DMA((1,)),
            pltpu.SemaphoreType.DMA((2,)),
            pltpu.SemaphoreType.DMA((chunks, n_inp - 1)),
            pltpu.SemaphoreType.DMA((chunks, n_inp - 1)),
            pltpu.SemaphoreType.DMA((chunks,)),
            pltpu.SemaphoreType.DMA((ch_dev, n_tm - 1)),
            pltpu.SemaphoreType.DMA((ch_dev, n_tm - 1)),
            pltpu.SemaphoreType.DMA((inputs // LANES,)),
        ],
        compiler_params=pltpu.CompilerParams(
            collective_id=0, has_side_effects=True, vmem_limit_bytes=63 << 20
        ),
    )(frames, tap_weights, jnp.asarray(tables(frame)))
    return mine.reshape(rows, 2, ch_dev, inputs)


def solution(mesh):
    return jax.shard_map(
        per_device,
        mesh=mesh,
        in_specs=(P("inp", "tm"), P()),
        out_specs=P("tm", None, "inp", None),
        check_vma=False,
    )
```

time: 387 us -> 316 us (0.82)
  local copies, waits for them, and re-layouts: 31.6 us -> 4.79 us
  matrix products: 23.6 us -> 0 us
  other arithmetic: 15 us -> 0 us
  waiting for transfers between devices: 4.6 us -> 0 us
    dot_general x2 -> x0, matrix products: 23.6 us -> none  [per_device(): jnp.einsum('isn,nj->ijs', folded, jnp.asarray(table, jnp.float32), precis...]
    convert_element_type x2 -> x0, local copies, waits for them, and re-layouts: 15.6 us -> none  [per_device(): side = jnp.einsum('isn,nj->ijs', folded, jnp.asarray(table, jnp.float32),...]
    add x1 -> x0, other arithmetic: 15 us -> none  [filter_taps(): total + weights[tap][None, None, :] * extended[:, tap:tap + count, :].ast...]
    transpose x1 -> x0, local copies, waits for them, and re-layouts: 6.63 us -> none  [per_device(): return mine.transpose(2, 1, 0, 3)]
    ppermute x1 -> x0, waiting for transfers between devices: 4.6 us -> none  [passed_along(): return lax.ppermute(block, axis, route)]
    unnamed x7 -> x1, local copies, waits for them, and re-layouts: 9.35 us -> 4.79 us
  transfers between devices with their start and end apart: 1 -> 0, of which waited for: 1 -> 0; matrix products, arithmetic and copies ran while one was open for 0% -> 0% of each run, Pallas kernels for 0% -> 0%
where the time goes in v1:
time: 316 us; the launch traced here: 312 us
  Pallas kernels  307 us (97%)
  local copies, waits for them, and re-layouts  4.79 us (2%)
    pallas_call x1, Pallas kernels, per_device(): pl.pallas_call(functools.partial(correlator, n_inp, n_tm, scale), out_sha...  307 us

profile of v1, /device:TPU:28, one launch (start us, length us, event | category | flops | bytes accessed | tf_op | source)
XLA Modules:
  0.0 312.2 jit_solution(5496541529864188418)
XLA Ops:
  0.0 307.4 %shard_map.37 = f32[4096,256]{1,0:T(8,128)} custom-call(bf16[4,384,8,512]{3,2,1,0:T(8,128)(2,1)} %bitcast.5, f32[4,512]{1,0:T(4,128)} %weights.1, bf16[2,256,768]{2,1,0:T(8,128)(2,1)} %constant.2.clone.table_hbm), custom_call_target="tpu_custom_call" | custom-call | tf_op jit(solution)/shard_map/pallas_call | solution.py:393
  307.4 4.8 %copy.5 = f32[64,2,32,256]{3,2,1,0:T(8,128)} copy(f32[64,2,32,256]{3,2,1,0:T(8,128)} %bitcast.4) | data formatting | bytes 8388608

commit v2 on v1

--- a/solution.py
+++ b/solution.py
@@ -12,9 +12,11 @@
 MESH = pl.DeviceIdType.MESH
 HEAD = 4
 STEPS = 32
-AHEAD = 10
-LAG = 3
-RING = 8
+OUTER = 2
+INNER = 8
+LATE = 8
+SOON = 2
+RING = 12
 LANES = 128
 
 
@@ -310,6 +312,11 @@
                 at = pl.ds(p * ch_dev + ch, rows, stride=2 * ch_dev)
                 held[t, at, :] = total[:, t * LANES : (t + 1) * LANES]
 
+    def done(g):
+        early = g + 1 - LATE
+        late = ch_dev - SOON - 2 * (ch_dev - 1 - g)
+        return jnp.maximum(jnp.maximum(early, late), 0)
+
     def channel(g):
         @pl.when(g >= RING)
         def _():
@@ -318,27 +325,26 @@
         correlate(g)
         each(1, n_tm, lambda d: sum_copy(g, d).start())
 
-        @pl.when(g >= LAG)
-        def _():
-            finish(g - LAG)
-
-    for c in range(1, min(AHEAD, chunks)):
-        send(c)
+        each(done(g - 1), done(g), finish)
+
+    ring = me // max(n_inp // 4, 1)
+    ahead = jnp.where(jnp.logical_and(ring > 0, ring < 3), INNER, OUTER)
+    each(1, jnp.minimum(ahead, chunks), send)
     own_head().wait()
     each(1, n_inp, lambda mask: head_copy(mask).wait_recv())
     each(0, head, channel)
 
     def step(c):
-        @pl.when(c + AHEAD - 1 < chunks)
-        def _():
-            send(c + AHEAD - 1)
+        @pl.when(c + ahead - 1 < chunks)
+        def _():
+            send(c + ahead - 1)
 
         own_copy(c).wait()
         each(1, n_inp, lambda mask: chunk_copy(c, mask).wait_recv())
         each(0, per, lambda k: channel(head + (c - 1) * per + k))
 
     each(1, chunks, step)
-    each(max(ch_dev - LAG, 0), ch_dev, finish)
+    each(done(ch_dev - 1), ch_dev, finish)
     out_copies = [
         pltpu.make_async_copy(held.at[t], out.at[:, pl.ds(t * LANES, LANES)], out_sem.at[t])
         for t in range(inputs // LANES)

time: 316 us -> 304 us (0.962); the launches traced: 312 us -> 304 us
  Pallas kernels: 307 us -> 299 us
    pallas_call x1, Pallas kernels: 307 us -> 299 us  [per_device(): pl.pallas_call(functools.partial(correlator, n_inp, n_tm, scale), out_sha...]
where the time goes in v2:
time: 304 us
  Pallas kernels  299 us (98%)
  local copies, waits for them, and re-layouts  4.79 us (2%)
    pallas_call x1, Pallas kernels, per_device(): pl.pallas_call(functools.partial(correlator, n_inp, n_tm, scale), out_sha...  299 us

profile of v2, /device:TPU:28, one launch (start us, length us, event | category | flops | bytes accessed | tf_op | source)
XLA Modules:
  0.0 303.5 jit_solution(2519084604434564473)
XLA Ops:
  0.0 298.7 %shard_map.37 = f32[4096,256]{1,0:T(8,128)} custom-call(bf16[4,384,8,512]{3,2,1,0:T(8,128)(2,1)} %bitcast.5, f32[4,512]{1,0:T(4,128)} %weights.1, bf16[2,256,768]{2,1,0:T(8,128)(2,1)} %constant.2.clone.table_hbm), custom_call_target="tpu_custom_call" | custom-call | tf_op jit(solution)/shard_map/pallas_call | solution.py:399
  298.7 4.8 %copy.5 = f32[64,2,32,256]{3,2,1,0:T(8,128)} copy(f32[64,2,32,256]{3,2,1,0:T(8,128)} %bitcast.4) | data formatting | bytes 8388608

commit v3 on v2

--- a/solution.py
+++ b/solution.py
@@ -12,7 +12,7 @@
 MESH = pl.DeviceIdType.MESH
 HEAD = 4
 STEPS = 32
-OUTER = 2
+OUTER = 1
 INNER = 8
 LATE = 8
 SOON = 2
@@ -207,21 +207,30 @@
             for n in range(2):
                 turn[pl.ds(2 * k + n, half, stride=width), :] = side[:, n * block : (n + 1) * block]
 
-        each(0, width // 2, pair)
+        def several(k):
+            for n in range(together):
+                pair(together * k + n)
+
+        pairs = width // 2
+        together = math.gcd(pairs, 4)
+        each(0, pairs // together, several)
 
     def spread(u, odd):
         g, s = place(u)
         at = pl.ds(pl.multiple_of(g * width, width), width)
         span = pl.ds(pl.multiple_of(s * block, block), block)
-        size = 2 * width
+        lot = math.gcd(fold, 8)
+        lots = fold // lot
+        size = lot * 2 * width
 
         def some(k):
             rows_in = turn[pl.ds(pl.multiple_of(k * size, size), size), :]
-            spec[k // fold, odd * fold + lax.rem(k, fold), :, at, span] = rows_in.astype(
-                jnp.bfloat16
-            ).reshape(2, width, block)
-
-        each(0, n_inp * fold, some)
+            to = pl.ds(odd * fold + lax.rem(k, lots) * lot, lot)
+            spec[k // lots, to, :, at, span] = rows_in.astype(jnp.bfloat16).reshape(
+                lot, 2, width, block
+            )
+
+        each(0, n_inp * lots, some)
 
     def unit(u):
         @pl.when(u + 1 < units)

time: 304 us -> 300 us (0.987)
  Pallas kernels: 299 us -> 294 us
    pallas_call x1, Pallas kernels: 299 us -> 294 us  [per_device(): pl.pallas_call(functools.partial(correlator, n_inp, n_tm, scale), out_sha...]
where the time goes in v3:
time: 300 us; the launch traced here: 299 us
  Pallas kernels  294 us (98%)
  local copies, waits for them, and re-layouts  4.79 us (2%)
    pallas_call x1, Pallas kernels, per_device(): pl.pallas_call(functools.partial(correlator, n_inp, n_tm, scale), out_sha...  294 us

profile of v3, /device:TPU:28, one launch (start us, length us, event | category | flops | bytes accessed | tf_op | source)
XLA Modules:
  0.0 298.6 jit_solution(2607273268024044117)
XLA Ops:
  0.0 293.8 %shard_map.37 = f32[4096,256]{1,0:T(8,128)} custom-call(bf16[4,384,8,512]{3,2,1,0:T(8,128)(2,1)} %bitcast.5, f32[4,512]{1,0:T(4,128)} %weights.1, bf16[2,256,768]{2,1,0:T(8,128)(2,1)} %constant.2.clone.table_hbm), custom_call_target="tpu_custom_call" | custom-call | tf_op jit(solution)/shard_map/pallas_call | solution.py:408
  293.8 4.8 %copy.5 = f32[64,2,32,256]{3,2,1,0:T(8,128)} copy(f32[64,2,32,256]{3,2,1,0:T(8,128)} %bitcast.4) | data formatting | bytes 8388608

commit v4 on v3

--- a/solution.py
+++ b/solution.py
@@ -11,7 +11,9 @@
 
 MESH = pl.DeviceIdType.MESH
 HEAD = 4
-STEPS = 32
+MIDDLE = 32
+LAST = 32
+TAIL = 8
 OUTER = 1
 INNER = 8
 LATE = 8
@@ -39,10 +41,19 @@
     return peer, peer
 
 
+def plan(ch_dev):
+    head = max(ch_dev // HEAD, 1)
+    tail = max(ch_dev // TAIL, 1)
+    big = math.gcd(max(ch_dev // MIDDLE, 1), ch_dev - head - tail)
+    per = math.gcd(max(ch_dev // LAST, 1), tail)
+    bigs = (ch_dev - head - tail) // big
+    return head, big, bigs, per, 1 + bigs + tail // per
+
+
 def correlator(
-    n_inp, n_tm, scale, x, weights, table_hbm, out,
-    xb, halo, table, low, high, turn, spec, recv, part, got, held,
-    x_sem, table_sem, halo_sem, send_sem, recv_sem, own_sem, put_sem, got_sem, out_sem,
+    n_inp, n_tm, scale, x, weights, table_hbm, held,
+    xb, halo, table, low, high, turn, spec, recv, part, got,
+    x_sem, table_sem, halo_sem, send_sem, recv_sem, put_sem, got_sem,
 ):
     me = lax.axis_index("inp")
     seg = lax.axis_index("tm")
@@ -56,9 +67,7 @@
     fold = ch_dev // 2
     inputs = n_inp * in_dev
     rows = inputs // n_tm
-    head = max(ch_dev // HEAD, 1)
-    per = max(ch_dev // STEPS, 1)
-    chunks = 1 + (ch_dev - head) // per
+    head, big, bigs, per, chunks = plan(ch_dev)
     in_units = in_dev // width
     s_units = count // block
     units = in_units * s_units
@@ -119,21 +128,26 @@
 
     def own_head():
         return pltpu.make_async_copy(
-            spec.at[me, pl.ds(0, head)], recv.at[pl.ds(0, head), :, me], own_sem.at[0]
-        )
-
-    def own_copy(c):
-        chunk = pl.ds(head + (c - 1) * per, per)
+            spec.at[me, pl.ds(0, head)], recv.at[pl.ds(0, head), :, me], recv_sem.at[0]
+        )
+
+    def whole_chunk(c):
+        return pl.ds(head + (c - 1) * big, big)
+
+    def small_chunk(c):
+        return pl.ds(head + bigs * big + (c - 1 - bigs) * per, per)
+
+    def own_copy(c, chunk):
         return pltpu.make_async_copy(
-            spec.at[me, chunk], recv.at[chunk, :, me], own_sem.at[c]
+            spec.at[me, chunk], recv.at[chunk, :, me], recv_sem.at[c]
         )
 
     def remote(mask, c, src, dst):
         return pltpu.make_async_remote_copy(
             src_ref=src,
             dst_ref=dst,
-            send_sem=send_sem.at[c, mask - 1],
-            recv_sem=recv_sem.at[c, mask - 1],
+            send_sem=send_sem.at[0],
+            recv_sem=recv_sem.at[c],
             device_id={"inp": across(me, mask, n_inp)[0]},
             device_id_type=MESH,
         )
@@ -148,19 +162,29 @@
             mask, 0, spec.at[peer, first, :, at, span], recv.at[first, :, me, at, span]
         )
 
-    def head_copy(mask):
+    def take(c, chunk):
+        pltpu.make_async_copy(recv.at[chunk], recv.at[chunk], recv_sem.at[c]).wait()
+
+    def sent():
+        most = spec.at[pl.ds(0, n_inp - 1)]
+        pltpu.make_async_copy(most, most, send_sem.at[0]).wait()
+
+    def chunk_copy(c, mask, chunk):
         peer = across(me, mask, n_inp)[0]
-        first = pl.ds(0, head)
-        return remote(mask, 0, spec.at[peer, first], recv.at[first, :, me])
-
-    def chunk_copy(c, mask):
-        peer = across(me, mask, n_inp)[0]
-        chunk = pl.ds(head + (c - 1) * per, per)
         return remote(mask, c, spec.at[peer, chunk], recv.at[chunk, :, me])
 
+    def send_chunk(c, chunk):
+        own_copy(c, chunk).start()
+        each(0, n_inp - 1, lambda k: chunk_copy(c, n_inp - 1 - k, chunk).start())
+
     def send(c):
-        own_copy(c).start()
-        each(0, n_inp - 1, lambda k: chunk_copy(c, n_inp - 1 - k).start())
+        @pl.when(c <= bigs)
+        def _():
+            send_chunk(c, whole_chunk(c))
+
+        @pl.when(c > bigs)
+        def _():
+            send_chunk(c, small_chunk(c))
 
     def filter_unit(u):
         slot = lax.rem(u, 2)
@@ -285,8 +309,8 @@
         return pltpu.make_async_remote_copy(
             src_ref=part.at[lax.rem(g, RING), peer],
             dst_ref=got.at[d - 1, g],
-            send_sem=put_sem.at[g, d - 1],
-            recv_sem=got_sem.at[g, d - 1],
+            send_sem=put_sem.at[lax.rem(g, RING)],
+            recv_sem=got_sem.at[g],
             device_id={"tm": peer},
             device_id_type=MESH,
         )
@@ -309,8 +333,14 @@
             for q in range(n_tm):
                 part[lax.rem(ch, RING), q, p] = product[q * rows : (q + 1) * rows]
 
+    def put(g):
+        slot = lax.rem(g, RING)
+        summed = part.at[slot, pl.ds(0, n_tm - 1)]
+        pltpu.make_async_copy(summed, summed, put_sem.at[slot]).wait()
+
     def finish(g):
-        each(1, n_tm, lambda d: sum_copy(g, d).wait_recv())
+        summed = got.at[:, g]
+        pltpu.make_async_copy(summed, summed, got_sem.at[g]).wait()
         ch = lax.rem(g, fold) * 2 + g // fold
         for p in range(2):
             total = part[lax.rem(g, RING), seg, p]
@@ -329,7 +359,7 @@
     def channel(g):
         @pl.when(g >= RING)
         def _():
-            each(1, n_tm, lambda d: sum_copy(g - RING, d).wait_send())
+            put(g - RING)
 
         correlate(g)
         each(1, n_tm, lambda d: sum_copy(g, d).start())
@@ -339,8 +369,7 @@
     ring = me // max(n_inp // 4, 1)
     ahead = jnp.where(jnp.logical_and(ring > 0, ring < 3), INNER, OUTER)
     each(1, jnp.minimum(ahead, chunks), send)
-    own_head().wait()
-    each(1, n_inp, lambda mask: head_copy(mask).wait_recv())
+    take(0, pl.ds(0, head))
     each(0, head, channel)
 
     def step(c):
@@ -348,26 +377,37 @@
         def _():
             send(c + ahead - 1)
 
-        own_copy(c).wait()
-        each(1, n_inp, lambda mask: chunk_copy(c, mask).wait_recv())
-        each(0, per, lambda k: channel(head + (c - 1) * per + k))
+        @pl.when(c <= bigs)
+        def _():
+            take(c, whole_chunk(c))
+
+        @pl.when(c > bigs)
+        def _():
+            take(c, small_chunk(c))
+
+        first = jnp.where(
+            c <= bigs, head + (c - 1) * big, head + bigs * big + (c - 1 - bigs) * per
+        )
+        each(0, jnp.where(c <= bigs, big, per), lambda k: channel(first + k))
 
     each(1, chunks, step)
     each(done(ch_dev - 1), ch_dev, finish)
-    out_copies = [
-        pltpu.make_async_copy(held.at[t], out.at[:, pl.ds(t * LANES, LANES)], out_sem.at[t])
-        for t in range(inputs // LANES)
-    ]
-    for copy in out_copies:
-        copy.start()
-    each(1, n_inp, lambda mask: head_copy(mask).wait_send())
-    each(1, chunks, lambda c: each(1, n_inp, lambda mask: chunk_copy(c, mask).wait_send()))
+    sent()
     each(
         max(ch_dev - RING, 0),
         ch_dev,
-        lambda g: each(1, n_tm, lambda d: sum_copy(g, d).wait_send()),
+        put,
     )
-    for copy in out_copies:
+
+
+def deliver(held, out, sem):
+    copies = [
+        pltpu.make_async_copy(held.at[t], out.at[:, pl.ds(t * LANES, LANES)], sem.at[t])
+        for t in range(held.shape[0])
+    ]
+    for copy in copies:
+        copy.start()
+    for copy in copies:
         copy.wait()
 
 
@@ -400,20 +440,19 @@
     groups = in_dev // 8
     pack = math.gcd(groups, 2)
     block = LANES
-    head = max(ch_dev // HEAD, 1)
-    per = max(ch_dev // STEPS, 1)
-    chunks = 1 + (ch_dev - head) // per
+    chunks = plan(ch_dev)[-1]
     scale = 1.0 / math.sqrt(count * n_tm)
+    tiles = inputs // LANES
     frames = samples.reshape(groups, 8, count, frame).transpose(0, 2, 1, 3)
     mine = pl.pallas_call(
         functools.partial(correlator, n_inp, n_tm, scale),
-        out_shape=jax.ShapeDtypeStruct((rows * 2 * ch_dev, inputs), jnp.float32),
+        out_shape=pltpu.VMEM((tiles, rows * 2 * ch_dev, LANES), jnp.float32),
         in_specs=[
             pl.BlockSpec(memory_space=pltpu.HBM),
             pl.BlockSpec(memory_space=pltpu.VMEM),
             pl.BlockSpec(memory_space=pltpu.HBM),
         ],
-        out_specs=pl.BlockSpec(memory_space=pltpu.HBM),
+        out_specs=pl.BlockSpec(memory_space=pltpu.VMEM),
         scratch_shapes=[
             pltpu.VMEM((2, pack, block + rim, 8, frame), jnp.bfloat16),
             pltpu.VMEM((groups, rim, 8, frame), jnp.bfloat16),
@@ -425,22 +464,27 @@
             pltpu.VMEM((ch_dev, 2, n_inp, in_dev, count), jnp.bfloat16),
             pltpu.VMEM((RING, n_tm, 2, rows, inputs), jnp.float32),
             pltpu.VMEM((n_tm - 1, ch_dev, 2, rows, inputs), jnp.float32),
-            pltpu.VMEM((inputs // LANES, rows * 2 * ch_dev, LANES), jnp.float32),
             pltpu.SemaphoreType.DMA((2,)),
             pltpu.SemaphoreType.DMA((1,)),
             pltpu.SemaphoreType.DMA((2,)),
-            pltpu.SemaphoreType.DMA((chunks, n_inp - 1)),
-            pltpu.SemaphoreType.DMA((chunks, n_inp - 1)),
+            pltpu.SemaphoreType.DMA((1,)),
             pltpu.SemaphoreType.DMA((chunks,)),
-            pltpu.SemaphoreType.DMA((ch_dev, n_tm - 1)),
-            pltpu.SemaphoreType.DMA((ch_dev, n_tm - 1)),
-            pltpu.SemaphoreType.DMA((inputs // LANES,)),
+            pltpu.SemaphoreType.DMA((RING,)),
+            pltpu.SemaphoreType.DMA((ch_dev,)),
         ],
         compiler_params=pltpu.CompilerParams(
-            collective_id=0, has_side_effects=True, vmem_limit_bytes=63 << 20
+            collective_id=0, has_side_effects=True, vmem_limit_bytes=58 << 20
         ),
     )(frames, tap_weights, jnp.asarray(tables(frame)))
-    return mine.reshape(rows, 2, ch_dev, inputs)
+    whole = pl.pallas_call(
+        deliver,
+        out_shape=jax.ShapeDtypeStruct((rows * 2 * ch_dev, inputs), jnp.float32),
+        in_specs=[pl.BlockSpec(memory_space=pltpu.VMEM)],
+        out_specs=pl.BlockSpec(memory_space=pltpu.HBM),
+        scratch_shapes=[pltpu.SemaphoreType.DMA((tiles,))],
+        compiler_params=pltpu.CompilerParams(vmem_limit_bytes=8 << 20),
+    )(pltpu.with_memory_space_constraint(mine, pltpu.VMEM))
+    return whole.reshape(rows, 2, ch_dev, inputs)
 
 
 def solution(mesh):

time: 300 us -> 291 us (0.970)
  local copies, waits for them, and re-layouts: 4.79 us -> 0 us
  Pallas kernels: 294 us -> 290 us
    pallas_call x1, Pallas kernels: 294 us -> 287 us  [per_device(): pl.pallas_call(functools.partial(correlator, n_inp, n_tm, scale), out_sha...]
    unnamed x1 -> x0, local copies, waits for them, and re-layouts: 4.79 us -> none
where the time goes in v4:
time: 291 us; the launch traced here: 290 us
  Pallas kernels  290 us (100%)
    pallas_call x1, Pallas kernels, per_device(): pl.pallas_call(functools.partial(correlator, n_inp, n_tm, scale), out_sha...  287 us

profile of v4, /device:TPU:28, one launch (start us, length us, event | category | flops | bytes accessed | tf_op | source)
XLA Modules:
  0.0 289.5 jit_solution(3284328624603834071)
XLA Ops:
  0.0 287.5 %shard_map.37.held = f32[2,4096,128]{2,1,0:T(8,128)S(1)} custom-call(bf16[4,384,8,512]{3,2,1,0:T(8,128)(2,1)} %bitcast.4, f32[4,512]{1,0:T(4,128)} %weights.1, bf16[2,256,768]{2,1,0:T(8,128)(2,1)} %constant.2.clone.table_hbm), custom_call_target="tpu_custom_call" | custom-call | tf_op jit(solution)/shard_map/pallas_call | solution.py:447
  287.5 2.0 shard_map.38

commit v5 on v4

--- a/solution.py
+++ b/solution.py
@@ -11,15 +11,14 @@
 
 MESH = pl.DeviceIdType.MESH
 HEAD = 4
-MIDDLE = 32
-LAST = 32
-TAIL = 8
+STEPS = 32
 OUTER = 1
 INNER = 8
 LATE = 8
 SOON = 2
 RING = 12
 LANES = 128
+PIECES = 1
 
 
 def each(first, end, body):
@@ -43,17 +42,14 @@
 
 def plan(ch_dev):
     head = max(ch_dev // HEAD, 1)
-    tail = max(ch_dev // TAIL, 1)
-    big = math.gcd(max(ch_dev // MIDDLE, 1), ch_dev - head - tail)
-    per = math.gcd(max(ch_dev // LAST, 1), tail)
-    bigs = (ch_dev - head - tail) // big
-    return head, big, bigs, per, 1 + bigs + tail // per
+    per = math.gcd(max(ch_dev // STEPS, 1), ch_dev - head)
+    return head, per, 1 + (ch_dev - head) // per
 
 
 def correlator(
-    n_inp, n_tm, scale, x, weights, table_hbm, held,
-    xb, halo, table, low, high, turn, spec, recv, part, got,
-    x_sem, table_sem, halo_sem, send_sem, recv_sem, put_sem, got_sem,
+    n_inp, n_tm, scale, x, weights_hbm, table_hbm, held,
+    weights, xb, halo, table, low, high, turn, spec, recv, part, got,
+    weights_sem, x_sem, table_sem, halo_sem, send_sem, recv_sem, put_sem, got_sem,
 ):
     me = lax.axis_index("inp")
     seg = lax.axis_index("tm")
@@ -67,50 +63,44 @@
     fold = ch_dev // 2
     inputs = n_inp * in_dev
     rows = inputs // n_tm
-    head, big, bigs, per, chunks = plan(ch_dev)
+    head, per, chunks = plan(ch_dev)
     in_units = in_dev // width
     s_units = count // block
     units = in_units * s_units
 
-    barrier = pltpu.get_barrier_semaphore()
-    for d in range(1, n_inp):
-        pl.semaphore_signal(
-            barrier, inc=1, device_id={"inp": lax.rem(me + d, n_inp)}, device_id_type=MESH
-        )
-    for d in range(1, n_tm):
-        pl.semaphore_signal(
-            barrier, inc=1, device_id={"tm": lax.rem(seg + d, n_tm)}, device_id_type=MESH
-        )
-
     def place(u):
         return lax.rem(u, in_units), lax.rem(u // in_units + 1, s_units)
 
-    def inner_load(u):
+    def inner_load(u, n):
         g, s = place(u)
         slot = lax.rem(u, 2)
         return pltpu.make_async_copy(
-            x.at[pl.ds(g * pack, pack), pl.ds(s * block - rim, block + rim)],
-            xb.at[slot], x_sem.at[slot],
-        )
-
-    def first_load(u):
+            x.at[g * pack + n, pl.ds(s * block - rim, block + rim)],
+            xb.at[slot, n], x_sem.at[slot, n],
+        )
+
+    def first_load(u, n):
         g, _ = place(u)
         slot = lax.rem(u, 2)
         return pltpu.make_async_copy(
-            x.at[pl.ds(g * pack, pack), pl.ds(0, block)],
-            xb.at[slot, :, pl.ds(rim, block)], x_sem.at[slot],
-        )
-
-    def load(u, act):
+            x.at[g * pack + n, pl.ds(0, block)],
+            xb.at[slot, n, pl.ds(rim, block)], x_sem.at[slot, n],
+        )
+
+    def load(u, n, act):
         _, s = place(u)
 
         @pl.when(s > 0)
         def _():
-            act(inner_load(u))
+            act(inner_load(u, n))
 
         @pl.when(s == 0)
         def _():
-            act(first_load(u))
+            act(first_load(u, n))
+
+    def load_all(u):
+        for n in range(pack):
+            load(u, n, lambda copy: copy.start())
 
     def rim_copy():
         return pltpu.make_async_remote_copy(
@@ -122,8 +112,20 @@
             device_id_type=MESH,
         )
 
+    weights_copy = pltpu.make_async_copy(weights_hbm, weights, weights_sem.at[0])
+    weights_copy.start()
+    load_all(0)
+    barrier = pltpu.get_barrier_semaphore()
+    for d in range(1, n_inp):
+        pl.semaphore_signal(
+            barrier, inc=1, device_id={"inp": lax.rem(me + d, n_inp)}, device_id_type=MESH
+        )
+    for d in range(1, n_tm):
+        pl.semaphore_signal(
+            barrier, inc=1, device_id={"tm": lax.rem(seg + d, n_tm)}, device_id_type=MESH
+        )
+
     table_copy = pltpu.make_async_copy(table_hbm, table, table_sem.at[0])
-    load(0, lambda copy: copy.start())
     table_copy.start()
 
     def own_head():
@@ -131,15 +133,12 @@
             spec.at[me, pl.ds(0, head)], recv.at[pl.ds(0, head), :, me], recv_sem.at[0]
         )
 
-    def whole_chunk(c):
-        return pl.ds(head + (c - 1) * big, big)
-
-    def small_chunk(c):
-        return pl.ds(head + bigs * big + (c - 1 - bigs) * per, per)
-
-    def own_copy(c, chunk):
+    def channels(c):
+        return pl.ds(head + (c - 1) * per, per)
+
+    def own_copy(c):
         return pltpu.make_async_copy(
-            spec.at[me, chunk], recv.at[chunk, :, me], recv_sem.at[c]
+            spec.at[me, channels(c)], recv.at[channels(c), :, me], recv_sem.at[c]
         )
 
     def remote(mask, c, src, dst):
@@ -169,30 +168,27 @@
         most = spec.at[pl.ds(0, n_inp - 1)]
         pltpu.make_async_copy(most, most, send_sem.at[0]).wait()
 
-    def chunk_copy(c, mask, chunk):
+    def chunk_copy(c, mask):
         peer = across(me, mask, n_inp)[0]
-        return remote(mask, c, spec.at[peer, chunk], recv.at[chunk, :, me])
-
-    def send_chunk(c, chunk):
-        own_copy(c, chunk).start()
-        each(0, n_inp - 1, lambda k: chunk_copy(c, n_inp - 1 - k, chunk).start())
+        return remote(mask, c, spec.at[peer, channels(c)], recv.at[channels(c), :, me])
+
+    def order(k):
+        if n_inp & (n_inp - 1) or n_inp < 4:
+            return n_inp - 1 - k
+        lot = n_inp // 4
+        far = n_inp - 1 - 2 * lax.rem(k, lot) - lax.rem(k // lot + me, 2)
+        return jnp.where(k < 2 * lot, far, n_inp - 1 - k)
 
     def send(c):
-        @pl.when(c <= bigs)
-        def _():
-            send_chunk(c, whole_chunk(c))
-
-        @pl.when(c > bigs)
-        def _():
-            send_chunk(c, small_chunk(c))
+        own_copy(c).start()
+        each(0, n_inp - 1, lambda k: chunk_copy(c, order(k)).start())
 
     def filter_unit(u):
         slot = lax.rem(u, 2)
         step = 8
 
-        def some(k):
-            g = k // (block // step)
-            s = lax.rem(k, block // step) * step
+        def some(g, k):
+            s = k * step
             to = pl.ds(pl.multiple_of((g * block + s) * 8, step * 8), step * 8)
             for t in range(half // LANES):
                 sides = []
@@ -206,9 +202,11 @@
                 low[t, to] = sides[0] + sides[1]
                 high[t, to] = sides[0] - sides[1]
 
-        each(0, pack * (block // step), some)
-
-    def transform(folded, odd):
+        for g in range(pack):
+            load(u, g, lambda copy: copy.wait())
+            each(0, block // step, functools.partial(some, g))
+
+    def transform(folded, odd, start, size):
         def pair(k):
             two = []
             for i in (2 * k, 2 * k + 1):
@@ -223,45 +221,50 @@
             top = value.astype(jnp.bfloat16)
             rest = (value - top.astype(jnp.float32)).astype(jnp.bfloat16)
             side = lax.dot_general(
-                table[odd],
+                table[odd, start : start + size],
                 jnp.concatenate([top, top, rest], axis=1),
                 (((1,), (1,)), ((), ())),
                 preferred_element_type=jnp.float32,
             )
             for n in range(2):
-                turn[pl.ds(2 * k + n, half, stride=width), :] = side[:, n * block : (n + 1) * block]
+                at = pl.ds(start * width + 2 * k + n, size, stride=width)
+                turn[at, :] = side[:, n * block : (n + 1) * block]
 
         def several(k):
             for n in range(together):
                 pair(together * k + n)
 
         pairs = width // 2
-        together = math.gcd(pairs, 4)
+        together = math.gcd(pairs, 8)
         each(0, pairs // together, several)
 
-    def spread(u, odd):
+    def spread(u, odd, start, size):
         g, s = place(u)
         at = pl.ds(pl.multiple_of(g * width, width), width)
         span = pl.ds(pl.multiple_of(s * block, block), block)
-        lot = math.gcd(fold, 8)
-        lots = fold // lot
-        size = lot * 2 * width
+        lot = size // (2 * n_inp)
+        to = pl.ds(odd * fold + start // (2 * n_inp), lot)
+        length = lot * 2 * width
 
         def some(k):
-            rows_in = turn[pl.ds(pl.multiple_of(k * size, size), size), :]
-            to = pl.ds(odd * fold + lax.rem(k, lots) * lot, lot)
-            spec[k // lots, to, :, at, span] = rows_in.astype(jnp.bfloat16).reshape(
-                lot, 2, width, block
-            )
-
-        each(0, n_inp * lots, some)
+            first = start * width + k * length
+            rows_in = turn[pl.ds(pl.multiple_of(first, length), length), :]
+            spec[k, to, :, at, span] = rows_in.astype(jnp.bfloat16).reshape(lot, 2, width, block)
+
+        each(0, n_inp, some)
+
+    front = 2 * n_inp * min(head, fold)
+
+    def spread_all(u, odd):
+        spread(u, odd, 0, front)
+        if front < half:
+            spread(u, odd, front, half - front)
 
     def unit(u):
         @pl.when(u + 1 < units)
         def _():
-            load(u + 1, lambda copy: copy.start())
-
-        load(u, lambda copy: copy.wait())
+            load_all(u + 1)
+
         g, s = place(u)
 
         @pl.when(s == 0)
@@ -276,26 +279,41 @@
 
             xb[lax.rem(u, 2), :, 0:rim] = halo[pl.ds(g * pack, pack)]
 
+        @pl.when(u == 0)
+        def _():
+            weights_copy.wait()
+
         filter_unit(u)
 
         @pl.when(u == 0)
         def _():
             table_copy.wait()
 
-        transform(low, 0)
-        spread(u, 0)
-
         @pl.when(u == 0)
         def _():
+            transform(low, 0, 0, front)
+            spread(u, 0, 0, front)
             pl.semaphore_wait(barrier, n_inp - 1 + n_tm - 1)
 
             @pl.when(seg + 1 < n_tm)
             def _():
                 rim_copy().start()
 
-        each(0, n_inp - 1, lambda k: unit_copy(u, n_inp - 1 - k).start())
-        transform(high, 1)
-        spread(u, 1)
+        @pl.when(u > 0)
+        def _():
+            transform(low, 0, 0, half)
+            spread_all(u, 0)
+
+        each(0, n_inp - 1, lambda k: unit_copy(u, order(k)).start())
+
+        @pl.when(u == 0)
+        def _():
+            if front < half:
+                transform(low, 0, front, half - front)
+                spread(u, 0, front, half - front)
+
+        transform(high, 1, 0, half)
+        spread_all(u, 1)
 
     each(0, units, unit)
     own_head().start()
@@ -304,11 +322,11 @@
     def _():
         rim_copy().wait_send()
 
-    def sum_copy(g, d):
-        peer = lax.rem(seg + d, n_tm)
+    def sum_copy(g, mask):
+        peer = across(seg, mask, n_tm)[0]
         return pltpu.make_async_remote_copy(
             src_ref=part.at[lax.rem(g, RING), peer],
-            dst_ref=got.at[d - 1, g],
+            dst_ref=got.at[mask - 1, g],
             send_sem=put_sem.at[lax.rem(g, RING)],
             recv_sem=got_sem.at[g],
             device_id={"tm": peer},
@@ -362,7 +380,7 @@
             put(g - RING)
 
         correlate(g)
-        each(1, n_tm, lambda d: sum_copy(g, d).start())
+        each(1, n_tm, lambda d: sum_copy(g, n_tm - d).start())
 
         each(done(g - 1), done(g), finish)
 
@@ -377,18 +395,8 @@
         def _():
             send(c + ahead - 1)
 
-        @pl.when(c <= bigs)
-        def _():
-            take(c, whole_chunk(c))
-
-        @pl.when(c > bigs)
-        def _():
-            take(c, small_chunk(c))
-
-        first = jnp.where(
-            c <= bigs, head + (c - 1) * big, head + bigs * big + (c - 1 - bigs) * per
-        )
-        each(0, jnp.where(c <= bigs, big, per), lambda k: channel(first + k))
+        take(c, channels(c))
+        each(0, per, lambda k: channel(head + (c - 1) * per + k))
 
     each(1, chunks, step)
     each(done(ch_dev - 1), ch_dev, finish)
@@ -401,9 +409,16 @@
 
 
 def deliver(held, out, sem):
+    tiles, length, _ = held.shape
+    piece = length // PIECES
     copies = [
-        pltpu.make_async_copy(held.at[t], out.at[:, pl.ds(t * LANES, LANES)], sem.at[t])
-        for t in range(held.shape[0])
+        pltpu.make_async_copy(
+            held.at[t, pl.ds(n * piece, piece)],
+            out.at[pl.ds(n * piece, piece), pl.ds(t * LANES, LANES)],
+            sem.at[t * PIECES + n],
+        )
+        for n in range(PIECES)
+        for t in range(tiles)
     ]
     for copy in copies:
         copy.start()
@@ -411,8 +426,11 @@
         copy.wait()
 
 
-def tables(frame):
+def tables(frame, n_inp, head):
     fold = frame // 2
+    columns = np.arange(fold).reshape(n_inp, fold // (2 * n_inp), 2)
+    parts = [columns[:, :head].reshape(-1), columns[:, head:].reshape(-1)]
+    order = np.concatenate(parts)
     sides = []
     for odd in (0, 1):
         column = np.arange(fold)
@@ -420,7 +438,7 @@
         phase = np.arange(fold)[:, None] * channel[None, :] % frame
         angle = phase * (2.0 * math.pi / frame)
         whole = np.where(column % 2 == 0, np.cos(angle), -np.sin(angle)) * frame ** (-0.5)
-        whole = whole.T.astype(np.float32)
+        whole = whole.T[order].astype(np.float32)
         top = whole.astype(jnp.bfloat16)
         rest = (whole - top.astype(np.float32)).astype(jnp.bfloat16)
         sides.append(np.concatenate([top, rest, top], axis=1))
@@ -449,11 +467,12 @@
         out_shape=pltpu.VMEM((tiles, rows * 2 * ch_dev, LANES), jnp.float32),
         in_specs=[
             pl.BlockSpec(memory_space=pltpu.HBM),
-            pl.BlockSpec(memory_space=pltpu.VMEM),
+            pl.BlockSpec(memory_space=pltpu.HBM),
             pl.BlockSpec(memory_space=pltpu.HBM),
         ],
         out_specs=pl.BlockSpec(memory_space=pltpu.VMEM),
         scratch_shapes=[
+            pltpu.VMEM((taps, frame), jnp.float32),
             pltpu.VMEM((2, pack, block + rim, 8, frame), jnp.bfloat16),
             pltpu.VMEM((groups, rim, 8, frame), jnp.bfloat16),
             pltpu.VMEM((2, frame // 2, 3 * (frame // 2)), jnp.bfloat16),
@@ -464,7 +483,8 @@
             pltpu.VMEM((ch_dev, 2, n_inp, in_dev, count), jnp.bfloat16),
             pltpu.VMEM((RING, n_tm, 2, rows, inputs), jnp.float32),
             pltpu.VMEM((n_tm - 1, ch_dev, 2, rows, inputs), jnp.float32),
-            pltpu.SemaphoreType.DMA((2,)),
+            pltpu.SemaphoreType.DMA((1,)),
+            pltpu.SemaphoreType.DMA((2, pack)),
             pltpu.SemaphoreType.DMA((1,)),
             pltpu.SemaphoreType.DMA((2,)),
             pltpu.SemaphoreType.DMA((1,)),
@@ -475,13 +495,13 @@
         compiler_params=pltpu.CompilerParams(
             collective_id=0, has_side_effects=True, vmem_limit_bytes=58 << 20
         ),
-    )(frames, tap_weights, jnp.asarray(tables(frame)))
+    )(frames, tap_weights, jnp.asarray(tables(frame, n_inp, plan(ch_dev)[0])))
     whole = pl.pallas_call(
         deliver,
         out_shape=jax.ShapeDtypeStruct((rows * 2 * ch_dev, inputs), jnp.float32),
         in_specs=[pl.BlockSpec(memory_space=pltpu.VMEM)],
         out_specs=pl.BlockSpec(memory_space=pltpu.HBM),
-        scratch_shapes=[pltpu.SemaphoreType.DMA((tiles,))],
+        scratch_shapes=[pltpu.SemaphoreType.DMA((tiles * PIECES,))],
         compiler_params=pltpu.CompilerParams(vmem_limit_bytes=8 << 20),
     )(pltpu.with_memory_space_constraint(mine, pltpu.VMEM))
     return whole.reshape(rows, 2, ch_dev, inputs)

time: 291 us -> 289 us (level); the launches traced: 290 us -> 285 us
  Pallas kernels: 290 us -> 285 us
    pallas_call x1, Pallas kernels: 287 us -> 283 us  [per_device(): pl.pallas_call(functools.partial(correlator, n_inp, n_tm, scale), out_sha...]
where the time goes in v5:
time: 289 us; the launch traced here: 285 us
  Pallas kernels  285 us (99%)
    pallas_call x1, Pallas kernels, per_device(): pl.pallas_call(functools.partial(correlator, n_inp, n_tm, scale), out_sha...  283 us

profile of v5, /device:TPU:28, one launch (start us, length us, event | category | flops | bytes accessed | tf_op | source)
XLA Modules:
  0.0 284.6 jit_solution(1227298729334114967)
XLA Ops:
  0.0 282.5 %shard_map.37.held = f32[2,4096,128]{2,1,0:T(8,128)S(1)} custom-call(bf16[4,384,8,512]{3,2,1,0:T(8,128)(2,1)} %bitcast.4, f32[4,512]{1,0:T(4,128)} %weights_hbm.1, bf16[2,256,768]{2,1,0:T(8,128)(2,1)} %constant.2.clone.table_hbm), custom_call_target="tpu_custom_call" | custom-call | tf_op jit(solution)/shard_map/pallas_call | solution.py:465
  282.6 2.0 shard_map.38

commit v6 on v5

--- a/solution.py
+++ b/solution.py
@@ -322,11 +322,11 @@
     def _():
         rim_copy().wait_send()
 
-    def sum_copy(g, mask):
+    def sum_copy(g, p, mask):
         peer = across(seg, mask, n_tm)[0]
         return pltpu.make_async_remote_copy(
-            src_ref=part.at[lax.rem(g, RING), peer],
-            dst_ref=got.at[mask - 1, g],
+            src_ref=part.at[lax.rem(g, RING), peer, p],
+            dst_ref=got.at[mask - 1, g, p],
             send_sem=put_sem.at[lax.rem(g, RING)],
             recv_sem=got_sem.at[g],
             device_id={"tm": peer},
@@ -338,6 +338,9 @@
         if in_dev % 16 == 0:
             return value.reshape(inputs, count)
         return value.astype(jnp.float32).reshape(inputs, count).astype(jnp.bfloat16)
+
+    def leave(ch, p, d):
+        sum_copy(ch, p, n_tm - d).start()
 
     def correlate(ch):
         real = side(ch, 0)
@@ -350,6 +353,7 @@
             )
             for q in range(n_tm):
                 part[lax.rem(ch, RING), q, p] = product[q * rows : (q + 1) * rows]
+            each(1, n_tm, functools.partial(leave, ch, p))
 
     def put(g):
         slot = lax.rem(g, RING)
@@ -380,7 +384,6 @@
             put(g - RING)
 
         correlate(g)
-        each(1, n_tm, lambda d: sum_copy(g, n_tm - d).start())
 
         each(done(g - 1), done(g), finish)
 

time: 289 us -> 288 us (level)
  no operation moved by 1% of the time
where the time goes in v6:
time: 288 us; the launch traced here: 285 us
  Pallas kernels  285 us (99%)
    pallas_call x1, Pallas kernels, per_device(): pl.pallas_call(functools.partial(correlator, n_inp, n_tm, scale), out_sha...  283 us

profile of v6, /device:TPU:28, one launch (start us, length us, event | category | flops | bytes accessed | tf_op | source)
XLA Modules:
  0.0 285.0 jit_solution(12862451308889725975)
XLA Ops:
  0.0 283.0 %shard_map.37.held = f32[2,4096,128]{2,1,0:T(8,128)S(1)} custom-call(bf16[4,384,8,512]{3,2,1,0:T(8,128)(2,1)} %bitcast.4, f32[4,512]{1,0:T(4,128)} %weights_hbm.1, bf16[2,256,768]{2,1,0:T(8,128)(2,1)} %constant.2.clone.table_hbm), custom_call_target="tpu_custom_call" | custom-call | tf_op jit(solution)/shard_map/pallas_call | solution.py:468
  283.0 2.0 shard_map.38

commit v7 on v6

--- a/solution.py
+++ b/solution.py
@@ -13,7 +13,7 @@
 HEAD = 4
 STEPS = 32
 OUTER = 1
-INNER = 8
+INNER = 3
 LATE = 8
 SOON = 2
 RING = 12

time: 288 us -> 288 us (level)
  no operation moved by 1% of the time
where the time goes in v7:
time: 288 us; the launch traced here: 285 us
  Pallas kernels  285 us (99%)
    pallas_call x1, Pallas kernels, per_device(): pl.pallas_call(functools.partial(correlator, n_inp, n_tm, scale), out_sha...  283 us

profile of v7, /device:TPU:28, one launch (start us, length us, event | category | flops | bytes accessed | tf_op | source)
XLA Modules:
  0.0 285.1 jit_solution(4044964453661437786)
XLA Ops:
  0.0 283.0 %shard_map.37.held = f32[2,4096,128]{2,1,0:T(8,128)S(1)} custom-call(bf16[4,384,8,512]{3,2,1,0:T(8,128)(2,1)} %bitcast.4, f32[4,512]{1,0:T(4,128)} %weights_hbm.1, bf16[2,256,768]{2,1,0:T(8,128)(2,1)} %constant.2.clone.table_hbm), custom_call_target="tpu_custom_call" | custom-call | tf_op jit(solution)/shard_map/pallas_call | solution.py:468
  283.0 2.0 shard_map.38

commit v8 on v7

--- a/solution.py
+++ b/solution.py
@@ -13,9 +13,9 @@
 HEAD = 4
 STEPS = 32
 OUTER = 1
-INNER = 3
+INNER = 2
 LATE = 8
-SOON = 2
+SOON = 1
 RING = 12
 LANES = 128
 PIECES = 1

time: 288 us -> 291 us (1.010)
  no operation moved by 1% of the time
where the time goes in v8:
time: 291 us; the launch traced here: 287 us
  Pallas kernels  287 us (99%)
    pallas_call x1, Pallas kernels, per_device(): pl.pallas_call(functools.partial(correlator, n_inp, n_tm, scale), out_sha...  285 us

profile of v8, /device:TPU:28, one launch (start us, length us, event | category | flops | bytes accessed | tf_op | source)
XLA Modules:
  0.0 287.2 jit_solution(1658956995755839747)
XLA Ops:
  0.0 285.2 %shard_map.37.held = f32[2,4096,128]{2,1,0:T(8,128)S(1)} custom-call(bf16[4,384,8,512]{3,2,1,0:T(8,128)(2,1)} %bitcast.4, f32[4,512]{1,0:T(4,128)} %weights_hbm.1, bf16[2,256,768]{2,1,0:T(8,128)(2,1)} %constant.2.clone.table_hbm), custom_call_target="tpu_custom_call" | custom-call | tf_op jit(solution)/shard_map/pallas_call | solution.py:468
  285.2 2.0 shard_map.38
